TPU v7x, 512 devices: a whole 4x4x16 slice. The times are simulated.
512 devices in a mesh: req: 64 (over x, z), head: 8 (over y, core).
Axes of the slice: x: 4, y: 4, z: 16, core: 2. Of those that a mesh axis runs over, the one named last changes fastest.
Arguments:
- tokens: bfloat16 [320, 1024], P('req'), may hold values from -6 to 6
- norm_gain: float32 [1024], replicated, may hold values from 0.1 to 1.9
- w_qkv: bfloat16 [1024, 8, 384], P(None, 'head'), may hold values from -0.1875 to 0.1875
- persist_kv: bfloat16 [8, 16, 256], P('head'), may hold values from -9 to 9
- memory: bfloat16 [64, 8, 128, 128], P('req', 'head'), may hold values from -0.5 to 0.5
- cache_kv: bfloat16 [512, 512, 8, 256], P('req', None, 'head')
- piece_owner: int32 [512], P('req'), may hold values from 0 to 63, as said below
- piece_len: int32 [512], P('req'), may hold values from 1 to 512, as said below
- w_out: bfloat16 [8, 128, 1024], P('head'), may hold values from -0.1875 to 0.1875
Outputs:
- layer_out: bfloat16 [320, 1024], P('req', 'head')
Inputs may be any that keep to these rules, and one draw needn't show every extreme that they name: `piece_owner`: every request owns 1 to 16 pieces, and one request owns exactly 16. `piece_len`: some piece is full.
All inputs are finite; a program needn't handle non-finite values.
Results may differ from a plain program's by a relative error of at most 0.009.
The roundings to bfloat16 on the way count: a program that leaves them out, or rounds other values in their place, can miss the bound.
Values may be sent and summed in bfloat16 or wider, within the bound.
No kernel may reach another device: no remote copies, remote signals or barrier semaphores. Data moves between devices by JAX's collectives and lax.ppermute only.
A program may use at most 64 MiB of HBM per device.

v0:
```python
import jax
import jax.numpy as jnp
from jax import lax
from jax.sharding import PartitionSpec as P

DH = 128
NP = 16
Q = 5
PIECE = 512
masked_score = -1e30
norm_eps = 1e-06


def merged(shard, axis, combine):
    everything = jax.tree.map(lambda part: lax.all_gather(part, axis), shard)
    leading = jax.tree.map(lambda part: part[0], everything)

    def step(k, so_far):
        return combine(so_far, jax.tree.map(lambda part: part[k], everything))

    return lax.fori_loop(1, lax.axis_size(axis), step, leading)


def join_parts(first, second):
    peak = jnp.maximum(first[0], second[0])
    scale_one = jnp.exp(first[0] - peak)
    scale_two = jnp.exp(second[0] - peak)
    total = first[1] * scale_one + second[1] * scale_two
    summed = first[2] * scale_one[..., None] + second[2] * scale_two[..., None]
    return (peak, total, summed)


def dense_parts(peaks, totals, summed, piece_owner, total_reqs):
    f32 = jnp.float32
    onehot = piece_owner[:, None] == jnp.arange(total_reqs, dtype=jnp.int32)[None, :]
    peak_dev = jnp.max(jnp.where(onehot[:, :, None, None], peaks[:, None], masked_score), axis=0)
    factor = jnp.exp(peaks - peak_dev[piece_owner])
    onehot_f = onehot.astype(f32)
    total_dev = jnp.einsum(
        "sr,shq->rhq", onehot_f, totals * factor, precision=lax.Precision.HIGHEST
    )
    summed_dev = jnp.einsum(
        "sr,shqe->rhqe", onehot_f, summed * factor[..., None], precision=lax.Precision.HIGHEST
    )
    return (peak_dev, total_dev, summed_dev)


def shards(tokens, norm_gain, w_qkv, persist_kv, memory, cache_kv, piece_owner, piece_len, w_out):
    f32 = jnp.float32
    rows = tokens.shape[0]
    heads = w_qkv.shape[1]
    req_dev = memory.shape[0]
    xf = tokens.astype(f32)
    normed = (
        xf * lax.rsqrt(jnp.mean(xf * xf, axis=-1, keepdims=True) + norm_eps) * norm_gain
    ).astype(jnp.bfloat16)
    proj = jnp.einsum("td,dhe->the", normed, w_qkv, preferred_element_type=f32)
    query = (proj[..., :DH] * DH ** (-0.5)).astype(jnp.bfloat16)
    new_key = proj[..., DH : 2 * DH].astype(jnp.bfloat16)
    new_value = proj[..., 2 * DH :].astype(jnp.bfloat16)
    all_query = lax.all_gather(query, "req", axis=0, tiled=True)
    query_all4 = all_query.reshape(-1, Q, heads, DH)
    total_reqs = query_all4.shape[0]
    query_rows = query_all4[piece_owner]
    scores = jnp.einsum(
        "sqhe,skhe->shqk", query_rows, cache_kv[..., :DH], preferred_element_type=f32
    )
    valid = (jnp.arange(PIECE)[None, :] < piece_len[:, None])[:, None, None, :]
    scores = jnp.where(valid, scores, masked_score)
    peaks = jnp.max(scores, axis=-1)
    weight = jnp.where(valid, jnp.exp(scores - peaks[..., None]), 0.0)
    totals = jnp.sum(weight, axis=-1)
    summed = jnp.einsum(
        "shqk,skhe->shqe",
        weight.astype(jnp.bfloat16),
        cache_kv[..., DH:],
        preferred_element_type=f32,
    )
    peak_dev, total_dev, summed_dev = dense_parts(peaks, totals, summed, piece_owner, total_reqs)
    peak_all, total_all, summed_all = merged((peak_dev, total_dev, summed_dev), "req", join_parts)
    start = lax.axis_index("req") * req_dev
    peak_cache = lax.dynamic_slice_in_dim(peak_all, start, req_dev, 0)
    total_cache = lax.dynamic_slice_in_dim(total_all, start, req_dev, 0)
    summed_cache = lax.dynamic_slice_in_dim(summed_all, start, req_dev, 0)
    query4 = query.reshape(req_dev, Q, heads, DH)
    key4 = new_key.reshape(req_dev, Q, heads, DH)
    value4 = new_value.reshape(req_dev, Q, heads, DH)
    score_persist = jnp.einsum(
        "rqhe,hne->rhqn", query4, persist_kv[..., :DH], preferred_element_type=f32
    )
    score_new = jnp.einsum("rqhe,rkhe->rhqk", query4, key4, preferred_element_type=f32)
    causal = jnp.arange(Q)[:, None] >= jnp.arange(Q)[None, :]
    score_new = jnp.where(causal, score_new, masked_score)
    score_own = jnp.concatenate([score_persist, score_new], axis=-1)
    peak_own = jnp.max(score_own, axis=-1)
    weight_own = jnp.exp(score_own - peak_own[..., None])
    total_own = jnp.sum(weight_own, axis=-1)
    rounded_own = weight_own.astype(jnp.bfloat16)
    summed_own = jnp.einsum(
        "rhqn,hne->rhqe", rounded_own[..., :NP], persist_kv[..., DH:], preferred_element_type=f32
    )
    summed_own = summed_own + jnp.einsum(
        "rhqk,rkhe->rhqe", rounded_own[..., NP:], value4, preferred_element_type=f32
    )
    peak_total = jnp.maximum(peak_cache, peak_own)
    scale_cache = jnp.exp(peak_cache - peak_total)
    scale_own = jnp.exp(peak_own - peak_total)
    total_final = total_cache * scale_cache + total_own * scale_own
    summed_final = summed_cache * scale_cache[..., None] + summed_own * scale_own[..., None]
    attended = summed_final / total_final[..., None]
    recalled = jnp.einsum("rqhe,rhef->rhqf", query4, memory, preferred_element_type=f32)
    head_out = (attended + recalled).astype(jnp.bfloat16)
    head_out = jnp.transpose(head_out, (0, 2, 1, 3)).reshape(rows, heads, DH)
    partial_out = jnp.einsum("thd,hdf->tf", head_out, w_out, preferred_element_type=f32)
    return lax.psum_scatter(partial_out, "head", scatter_dimension=1, tiled=True).astype(
        jnp.bfloat16
    )


def solution(mesh):
    in_specs = (
        P("req", None),
        P(),
        P(None, "head", None),
        P("head", None, None),
        P("req", "head", None, None),
        P("req", None, "head", None),
        P("req"),
        P("req"),
        P("head", None, None),
    )
    out_specs = P("req", "head")
    return jax.shard_map(shards, mesh=mesh, in_specs=in_specs, out_specs=out_specs, check_vma=False)
```

profile of v0, /device:TPU:2, one launch (start us, length us, event | category | flops | bytes accessed | tf_op | source)
XLA Modules:
  0.0 403.9 jit_solution(6034953627705232493)
XLA Ops:
  9.0 0.9 fusion.60
  10.0 88.1 %all_gather.21 = bf16[320,1,128]{2,1,0:T(2,128)(2,1)S(1)} all-gather(bf16[5,1,128]{2,1,0:T(2,128)(2,1)S(1)} %copy.57), channel_id=1, replica_groups=mesh['req'=64,'head'=8] {'req'}, dimensions={0}, use_global_device_ids=true | all-gather | bytes 83200 | tf_op jit(solution)/shard_map/all_gather | solution.py:61
  100.0 1.7 fusion.61
  102.8 1.0 fusion.25
  103.9 79.7 %all-gather.3 = f32[64,64,5]{1,2,0:T(8,128)S(1)} all-gather(f32[1,64,5]{1,2,0:T(8,128)S(1)} %bitcast.171), channel_id=2, replica_groups=mesh['req'=64,'head'=8] {'req'}, dimensions={0}, use_global_device_ids=true | all-gather | bytes 83200 | tf_op jit(solution)/shard_map/all_gather | solution.py:15
  184.0 81.1 %all-gather.4 = f32[64,64,5]{1,2,0:T(8,128)S(1)} all-gather(f32[1,64,5]{1,2,0:T(8,128)S(1)} %convolution_bitcast_fusion.1), channel_id=3, replica_groups=mesh['req'=64,'head'=8] {'req'}, dimensions={0}, use_global_device_ids=true | all-gather | bytes 83200 | tf_op jit(solution)/shard_map/all_gather | solution.py:15
  266.9 93.1 %while.19 = (s32[]{:T(128)}, f32[64,1,5]{0,1,2:T(1,128)S(1)}, f32[64,1,5]{0,1,2:T(1,128)S(1)}, f32[64,1,5,128]{3,2,1,0:T(8,128)S(1)}, f32[64,64,1,5]{1,2,3,0:T(1...) while((s32[]{:T(128)}, f32[64,1,5]{0,1,2:T(1,128)S(1)}, ...), condition=%wide.region_5.6_spmd, body=%wide.region_4.5_spmd.sunk | while | flops 124805 | bytes 837271 | solution.py:21
  267.0 0.9 constant_dynamic-slice_fusion.4
  268.5 0.9 constant_dynamic-slice_fusion.4
  270.0 0.9 constant_dynamic-slice_fusion.4
  271.4 0.9 constant_dynamic-slice_fusion.4
  272.9 0.9 constant_dynamic-slice_fusion.4
  274.4 0.9 constant_dynamic-slice_fusion.4
  275.9 0.9 constant_dynamic-slice_fusion.4
  277.4 0.9 constant_dynamic-slice_fusion.4
  278.8 0.9 constant_dynamic-slice_fusion.4
  280.3 0.9 constant_dynamic-slice_fusion.4
  281.8 0.9 constant_dynamic-slice_fusion.4
  283.3 0.9 constant_dynamic-slice_fusion.4
  284.7 0.9 constant_dynamic-slice_fusion.4
  286.2 0.9 constant_dynamic-slice_fusion.4
  287.7 0.9 constant_dynamic-slice_fusion.4
  289.2 0.9 constant_dynamic-slice_fusion.4
  290.7 0.9 constant_dynamic-slice_fusion.4
  292.1 0.9 constant_dynamic-slice_fusion.4
  293.6 0.9 constant_dynamic-slice_fusion.4
  295.1 0.9 constant_dynamic-slice_fusion.4
  301.0 0.9 constant_dynamic-slice_fusion.4
  329.1 0.9 constant_dynamic-slice_fusion.4
  357.2 0.9 constant_dynamic-slice_fusion.4
  361.7 34.1 %reduce-scatter.2.cloned.1.call-done = f32[5,128]{1,0:T(8,128)} async-done(((f32[5,1024]{1,0:T(8,128)}), f32[5,128]{1,0:T(8,128)}) %reduce-scatter.2.cloned.1.call-update) | async-done | bytes 2576 | tf_op jit(solution)/shard_map/reduce_scatter | solution.py:115
  395.8 1.2 convert_element_type.39
  (346 shorter events, 79.0 us)
Async XLA Ops:
  6.5 2.5 copy-start
  6.5 96.3 %copy-start.5 = (s32[8]{0:T(128)S(1)}, s32[8]{0:T(128)}, u32[]{:S(2)}) copy-start(s32[8]{0:T(128)} %param.17) | copy-start | bytes 100
  6.5 96.0 %copy-start.1 = (bf16[8,512,1,256]{3,1,2,0:T(8,128)(2,1)S(1)}, bf16[8,512,1,256]{3,1,2,0:T(8,128)(2,1)}, u32[]{:S(2)}) copy-start(bf16[8,512,1,256]{3,1,2,0:T(8,128)(2,1)} %param.16) | copy-start | bytes 6291460
  6.5 259.3 %all-gather.7.cloned.1.call-start = ((), (), s32[]{:S(2)}) async-start(), calls=%async_computation.2 | async-start | bytes 10649600 | tf_op jit(solution)/shard_map/all_gather | solution.py:15
  99.9 165.7 %copy-start.4 = (bf16[1,16,256]{2,1,0:T(8,128)(2,1)S(1)}, bf16[1,16,256]{2,1,0:T(8,128)(2,1)}, u32[]{:S(2)}) copy-start(bf16[1,16,256]{2,1,0:T(8,128)(2,1)} %param.14) | copy-start | bytes 24580
  103.9 291.9 %reduce-scatter.2.cloned.1.call-start = ((), (), s32[]{:S(2)}) async-start(), calls=%async_computation.1 | async-start | bytes 36864 | tf_op jit(solution)/shard_map/reduce_scatter | solution.py:115
  266.9 93.9 %copy-start.2 = (bf16[1,128,1024]{2,1,0:T(8,128)(2,1)S(1)}, bf16[1,128,1024]{2,1,0:T(8,128)(2,1)}, u32[]{:S(2)}) copy-start(bf16[1,128,1024]{2,1,0:T(8,128)(2,1)} %param.19) | copy-start | bytes 786436
  266.9 93.9 %copy-start.3 = (bf16[1,1,128,128]{3,2,1,0:T(8,128)(2,1)S(1)}, bf16[1,1,128,128]{3,2,1,0:T(8,128)(2,1)}, u32[]{:S(2)}) copy-start(bf16[1,1,128,128]{3,2,1,0:T(8,128)(2,1)} %param.15) | copy-start | bytes 98308
Sparse Core Ops, SparseCore 0:
  104.0 158.7 all-gather.6
  361.8 33.9 reduce-scatter.1
where the time goes:
time: 406 us; the launch traced here: 404 us
  blocking collectives  249 us (61%)
  local copies, waits for them, and re-layouts  74.2 us (18%)
  waiting for transfers between devices  34.2 us (8%)
  other arithmetic  25.4 us (6%)
  between operations  13.6 us (3%)
  matrix products  5.76 us (1%)
    all_gather x2, blocking collectives, merged(): everything = jax.tree.map(lambda part: lax.all_gather(part, axis), shard)  161 us
    all_gather x1, blocking collectives, shards(): all_query = lax.all_gather(query, 'req', axis=0, tiled=True)  88.1 us
    dynamic_slice x63, local copies, waits for them, and re-layouts, step(): return combine(so_far, jax.tree.map(lambda part: part[k], everything))  59.1 us
    reduce_scatter x1, waiting for transfers between devices, shards(): lax.psum_scatter(partial_out, 'head', scatter_dimension=1, tiled=True)  34.1 us
    add x63, other arithmetic, join_parts(): summed = first[2] * scale_one[..., None] + second[2] * scale_two[..., None]  17.9 us
    mul x126, local copies, waits for them, and re-layouts, join_parts(): summed = first[2] * scale_one[..., None] + second[2] * scale_two[..., None]  12.1 us
  transfers between devices with their start and end apart: 2, of which 1 were waited for; matrix products, arithmetic and copies ran while one was open for 0% of the time, Pallas kernels for 0%

commit v1 on v0

--- a/solution.py
+++ b/solution.py
@@ -58,7 +58,9 @@
     query = (proj[..., :DH] * DH ** (-0.5)).astype(jnp.bfloat16)
     new_key = proj[..., DH : 2 * DH].astype(jnp.bfloat16)
     new_value = proj[..., 2 * DH :].astype(jnp.bfloat16)
-    all_query = lax.all_gather(query, "req", axis=0, tiled=True)
+    all_query = jnp.concatenate(
+        lax.all_to_all(jnp.stack([query] * lax.axis_size("req")), "req", 0, 0), axis=0
+    )
     query_all4 = all_query.reshape(-1, Q, heads, DH)
     total_reqs = query_all4.shape[0]
     query_rows = query_all4[piece_owner]

time: 406 us -> 348 us (0.86)
  blocking collectives: 249 us -> 161 us
  starting transfers between devices: 0.04 us -> 18.7 us
  waiting for transfers between devices: 34.2 us -> 44.6 us
    all_gather x1 -> x0, blocking collectives: 88.1 us -> none  [shards(): all_query = lax.all_gather(query, 'req', axis=0, tiled=True)]
    all_to_all x0 -> x1, starting transfers between devices: none -> 18.6 us  [shards(): lax.all_to_all(jnp.stack([query] * lax.axis_size('req')), 'req', 0, 0)]
    all_to_all x0 -> x1, waiting for transfers between devices: none -> 13.3 us  [shards(): lax.all_to_all(jnp.stack([query] * lax.axis_size('req')), 'req', 0, 0)]
  transfers between devices with their start and end apart: 2 -> 3, of which waited for: 1 -> 2; matrix products, arithmetic and copies ran while one was open for 0% -> 1% of each run, Pallas kernels for 0% -> 0%
where the time goes in v1:
time: 348 us; the launch traced here: 346 us
  blocking collectives  161 us (46%)
  local copies, waits for them, and re-layouts  75.6 us (22%)
  waiting for transfers between devices  44.6 us (13%)
  other arithmetic  24.9 us (7%)
  starting transfers between devices  18.7 us (5%)
  between operations  13.6 us (4%)
  matrix products  5.77 us (2%)
    all_gather x2, blocking collectives, merged(): everything = jax.tree.map(lambda part: lax.all_gather(part, axis), shard)  161 us
    dynamic_slice x63, local copies, waits for them, and re-layouts, step(): return combine(so_far, jax.tree.map(lambda part: part[k], everything))  59.1 us
    reduce_scatter x1, waiting for transfers between devices, shards(): lax.psum_scatter(partial_out, 'head', scatter_dimension=1, tiled=True)  31.3 us
    all_to_all x1, starting transfers between devices, shards(): lax.all_to_all(jnp.stack([query] * lax.axis_size('req')), 'req', 0, 0)  18.6 us
    add x63, other arithmetic, join_parts(): summed = first[2] * scale_one[..., None] + second[2] * scale_two[..., None]  17.9 us
    all_to_all x1, waiting for transfers between devices, shards(): lax.all_to_all(jnp.stack([query] * lax.axis_size('req')), 'req', 0, 0)  13.3 us
    mul x126, local copies, waits for them, and re-layouts, join_parts(): summed = first[2] * scale_one[..., None] + second[2] * scale_two[..., None]  12.1 us
  transfers between devices with their start and end apart: 3, of which 2 were waited for; matrix products, arithmetic and copies ran while one was open for 1% of the time, Pallas kernels for 0%

profile of v1, /device:TPU:2, one launch (start us, length us, event | category | flops | bytes accessed | tf_op | source)
XLA Modules:
  0.0 346.1 jit_solution(5202365427208322558)
XLA Ops:
  6.5 1.0 fusion.20
  8.3 1.0 fusion.57
  10.0 18.6 %all-to-all-start = ((bf16[64,5,1,128]{3,1,2,0:T(8,128)(2,1)}), bf16[64,5,1,128]{3,1,2,0:T(8,128)(2,1)S(1)}, u32[]{:S(2)}, u32[]{:S(2)}) async-start(bf16[64,5,1,128]{3,1,2,0:T(8,128)(2,1)} %stack.2), calls=%async_computation | async-start | bytes 262144 | tf_op jit(solution)/shard_map/all_to_all | solution.py:62
  30.8 13.3 %all-to-all-done = bf16[64,5,1,128]{3,1,2,0:T(8,128)(2,1)S(1)} async-done(((bf16[64,5,1,128]{3,1,2,0:T(8,128)(2,1)}), bf16[64,5,1,128]{3,1,2,0:T(8,128)(2,1)S(1)}, u32[]{:S(2)}, u32[]{:S(2)}) %all-to-all-start) | async-done | bytes 81952 | tf_op jit(solution)/shard_map/all_to_all | solution.py:62
  44.7 1.7 fusion.58
  47.5 1.0 fusion.25
  49.1 80.0 %all-gather.3 = f32[64,64,5]{1,2,0:T(8,128)S(1)} all-gather(f32[1,64,5]{1,2,0:T(8,128)S(1)} %bitcast.166), channel_id=2, replica_groups=mesh['req'=64,'head'=8] {'req'}, dimensions={0}, use_global_device_ids=true | all-gather | bytes 83200 | tf_op jit(solution)/shard_map/all_gather | solution.py:15
  129.5 81.0 %all-gather.4 = f32[64,64,5]{1,2,0:T(8,128)S(1)} all-gather(f32[1,64,5]{1,2,0:T(8,128)S(1)} %convolution_bitcast_fusion.1), channel_id=3, replica_groups=mesh['req'=64,'head'=8] {'req'}, dimensions={0}, use_global_device_ids=true | all-gather | bytes 83200 | tf_op jit(solution)/shard_map/all_gather | solution.py:15
  212.0 93.1 %while.19 = (s32[]{:T(128)}, f32[64,1,5]{0,1,2:T(1,128)S(1)}, f32[64,1,5]{0,1,2:T(1,128)S(1)}, f32[64,1,5,128]{3,2,1,0:T(8,128)S(1)}, f32[64,64,1,5]{1,2,3,0:T(1...) while((s32[]{:T(128)}, f32[64,1,5]{0,1,2:T(1,128)S(1)}, ...), condition=%wide.region_5.6_spmd, body=%wide.region_4.5_spmd.sunk | while | flops 124805 | bytes 837271 | solution.py:21
  212.0 0.9 constant_dynamic-slice_fusion.4
  213.5 0.9 constant_dynamic-slice_fusion.4
  215.0 0.9 constant_dynamic-slice_fusion.4
  216.5 0.9 constant_dynamic-slice_fusion.4
  217.9 0.9 constant_dynamic-slice_fusion.4
  219.4 0.9 constant_dynamic-slice_fusion.4
  220.9 0.9 constant_dynamic-slice_fusion.4
  222.4 0.9 constant_dynamic-slice_fusion.4
  223.9 0.9 constant_dynamic-slice_fusion.4
  225.3 0.9 constant_dynamic-slice_fusion.4
  226.8 0.9 constant_dynamic-slice_fusion.4
  228.3 0.9 constant_dynamic-slice_fusion.4
  229.8 0.9 constant_dynamic-slice_fusion.4
  231.2 0.9 constant_dynamic-slice_fusion.4
  232.7 0.9 constant_dynamic-slice_fusion.4
  234.2 0.9 constant_dynamic-slice_fusion.4
  235.7 0.9 constant_dynamic-slice_fusion.4
  237.2 0.9 constant_dynamic-slice_fusion.4
  238.6 0.9 constant_dynamic-slice_fusion.4
  253.4 0.9 constant_dynamic-slice_fusion.4
  281.5 0.9 constant_dynamic-slice_fusion.4
  306.7 31.3 %reduce-scatter.2.cloned.1.call-done = f32[5,128]{1,0:T(8,128)} async-done(((f32[5,1024]{1,0:T(8,128)}), f32[5,128]{1,0:T(8,128)}) %reduce-scatter.2.cloned.1.call-update) | async-done | bytes 2576 | tf_op jit(solution)/shard_map/reduce_scatter | solution.py:117
  338.0 1.2 convert_element_type.42
  (345 shorter events, 80.8 us)
Async XLA Ops:
  6.5 1.8 copy-start
  6.5 41.0 %copy-start.5 = (s32[8]{0:T(128)S(1)}, s32[8]{0:T(128)}, u32[]{:S(2)}) copy-start(s32[8]{0:T(128)} %param.17) | copy-start | bytes 100
  6.5 40.7 %copy-start.1 = (bf16[8,512,1,256]{3,1,2,0:T(8,128)(2,1)S(1)}, bf16[8,512,1,256]{3,1,2,0:T(8,128)(2,1)}, u32[]{:S(2)}) copy-start(bf16[8,512,1,256]{3,1,2,0:T(8,128)(2,1)} %param.16) | copy-start | bytes 6291460
  8.3 40.6 %copy-start.4 = (bf16[1,16,256]{2,1,0:T(8,128)(2,1)S(1)}, bf16[1,16,256]{2,1,0:T(8,128)(2,1)}, u32[]{:S(2)}) copy-start(bf16[1,16,256]{2,1,0:T(8,128)(2,1)} %param.14) | copy-start | bytes 24580
  10.0 34.2 %all-to-all-start = ((bf16[64,5,1,128]{3,1,2,0:T(8,128)(2,1)}), bf16[64,5,1,128]{3,1,2,0:T(8,128)(2,1)S(1)}, u32[]{:S(2)}, u32[]{:S(2)}) async-start(bf16[64,5,1,128]{3,1,2,0:T(8,128)(2,1)} %stack.2), calls=%async_computation | async-start | bytes 262144 | tf_op jit(solution)/shard_map/all_to_all | solution.py:62
  28.6 182.3 %all-gather.7.cloned.1.call-start = ((), (), s32[]{:S(2)}) async-start(), calls=%async_computation.3 | async-start | bytes 10649600 | tf_op jit(solution)/shard_map/all_gather | solution.py:15
  48.6 289.4 %reduce-scatter.2.cloned.1.call-start = ((), (), s32[]{:S(2)}) async-start(), calls=%async_computation.2 | async-start | bytes 36864 | tf_op jit(solution)/shard_map/reduce_scatter | solution.py:117
  211.9 93.9 %copy-start.2 = (bf16[1,128,1024]{2,1,0:T(8,128)(2,1)S(1)}, bf16[1,128,1024]{2,1,0:T(8,128)(2,1)}, u32[]{:S(2)}) copy-start(bf16[1,128,1024]{2,1,0:T(8,128)(2,1)} %param.19) | copy-start | bytes 786436
  212.0 93.9 %copy-start.3 = (bf16[1,1,128,128]{3,2,1,0:T(8,128)(2,1)S(1)}, bf16[1,1,128,128]{3,2,1,0:T(8,128)(2,1)}, u32[]{:S(2)}) copy-start(bf16[1,1,128,128]{3,2,1,0:T(8,128)(2,1)} %param.15) | copy-start | bytes 98308
Sparse Core Ops, SparseCore 0:
  48.7 155.2 all-gather.6
  306.8 31.0 reduce-scatter.1
